TPU v7x, 32 devices: a whole 2x2x4 slice. The times are simulated.
32 devices in a mesh: band: 2 (over x), tm: 16 (over z, y, core).
Axes of the slice: x: 2, y: 2, z: 4, core: 2. Of those that a mesh axis runs over, the one named last changes fastest.
Arguments:
- voltages: bfloat16 [65536, 2048], P(('band', 'tm')), parts along dimension 0, may hold values from -6 to 6
- panel_map: int32 [2048], replicated, may hold values from 0 to 2047, each once
- block_list: int32 [16, 2], replicated, may hold values from 0 to 15, as said below
Outputs:
- visibilities: float32 [32, 2, 256, 128, 128], P('band', None, 'tm'), parts along dimension 0
There are 2 independent parts, one for each index of `band`. A program takes and returns all parts, laid end to end along the dimension named above; an argument that names none is the same for every part. Nothing has to cross between parts.
Inputs may be any that keep to these rules, and one draw needn't show every extreme that they name: `block_list`: each row is a pair of panel numbers; the list names exactly 8 distinct panels, among them panel 0 and panel 16 - 1, every one of them in its first column.
All inputs are finite; a program needn't handle non-finite values.
Results may differ from a plain program's by a relative error of at most 0.0064.
Values may be sent and summed in bfloat16 or wider, within the bound.
No kernel may reach another device: no remote copies, remote signals or barrier semaphores. Data moves between devices by JAX's collectives and lax.ppermute only.
A program may use at most 128 MiB of HBM per device.

v0:
```python
import jax
import jax.numpy as jnp
from jax import lax
from jax.sharding import PartitionSpec as P

CHANNELS = 256
TAPS = 4
PANEL = 128


def from_behind(block, axis, distance):
    devices = range(lax.axis_size(axis))
    route = [(i - distance, i) for i in devices if i - distance in devices]
    return lax.ppermute(block, axis, route)


def filter_taps(taps, frame):
    length = taps * frame
    place = jnp.arange(length).astype(jnp.float32)
    middle = (length - 1) / 2.0
    window = 0.5 - 0.5 * jnp.cos(2.0 * jnp.pi * (place + 0.5) / length)
    shape_h = jnp.sinc((place - middle) / frame) * window
    shape_h = shape_h / jnp.sqrt(jnp.sum(shape_h * shape_h))
    return shape_h.reshape(taps, frame).astype(jnp.float32)


def dft_table(channels):
    frame = 2 * channels
    rows_k = jnp.arange(channels, dtype=jnp.int32)[:, None]
    cols_n = jnp.arange(frame, dtype=jnp.int32)[None, :]
    phase = (rows_k * cols_n % frame).astype(jnp.float32) * (2.0 * jnp.pi / frame)
    return jnp.concatenate([jnp.cos(phase), -jnp.sin(phase)], axis=0).astype(jnp.bfloat16)


def body(voltages, panel_map, block_list):
    frame = 2 * CHANNELS
    spec_dev = voltages.shape[0] // frame
    groups = lax.axis_size("tm")
    band_dev = CHANNELS // groups
    panel_rows = panel_map.reshape(-1, PANEL)
    columns = panel_rows[block_list]
    width = voltages.shape[1]
    frames = voltages.reshape(spec_dev, frame, width)
    earlier = from_behind(frames[spec_dev - (TAPS - 1) :], "tm", 1)
    padded = jnp.concatenate([earlier, frames], axis=0)
    coeff = filter_taps(TAPS, frame)
    filtered = jnp.zeros((spec_dev, frame, width), jnp.float32)
    for tap in range(TAPS):
        filtered = filtered + coeff[tap][None, :, None] * padded[tap : tap + spec_dev].astype(
            jnp.float32
        )
    filtered = filtered.astype(jnp.bfloat16)
    table = dft_table(CHANNELS)
    spectra = jnp.einsum("kn,sni->ski", table, filtered, preferred_element_type=jnp.float32)
    spectra = spectra.astype(jnp.bfloat16).reshape(spec_dev, 2, groups, band_dev, width)
    data = lax.all_to_all(spectra, "tm", split_axis=2, concat_axis=0, tiled=True)[:, :, 0]
    total = data.shape[0]
    first = data[:, :, :, columns[:, 0]]
    second = data[:, :, :, columns[:, 1]]
    flipped = jnp.stack([first[:, 1], -first[:, 0]], axis=1)
    real_part = jnp.einsum("sckbi,sckbj->bkij", first, second, preferred_element_type=jnp.float32)
    imag_part = jnp.einsum("sckbi,sckbj->bkij", flipped, second, preferred_element_type=jnp.float32)
    return jnp.stack([real_part, imag_part], axis=1) / total


def solution(mesh):
    in_specs = (P(("band", "tm"), None), P(), P())
    out_specs = P("band", None, "tm", None, None)
    return jax.shard_map(body, mesh=mesh, in_specs=in_specs, out_specs=out_specs, check_vma=False)
```

profile of v0, /device:TPU:13, one launch (start us, length us, event | category | flops | bytes accessed | tf_op | source)
XLA Modules:
  0.0 472.7 jit_solution(12410593673535821267)
XLA Ops:
  0.0 0.0 copy-start
  0.0 6.6 %slice.44 = bf16[1536,2048]{1,0:T(8,128)(2,1)} slice(bf16[2048,2048]{1,0:T(8,128)(2,1)} %param.3), slice={[512:2048], [0:2048]} | slice | bytes 12582912 | tf_op jit(solution)/shard_map/slice | solution.py:44
  6.6 3.7 collective-permute-start
  10.3 0.6 multiply_reduce_fusion
  11.6 0.1 broadcast_divide_fusion
  11.6 2.2 negate_convert_fusion
  13.8 64.7 %collective-permute-done = bf16[3,512,2048]{2,1,0:T(8,128)(2,1)} collective-permute-done((bf16[3,512,2048]{2,1,0:T(8,128)(2,1)}, bf16[3,512,2048]{2,1,0:T(8,128)(2,1)}, u32[]{:S(2)}, u32[]{:S(2)}) %collective-permute-start) | collective-permute-done | bytes 6291488 | tf_op jit(solution)/shard_map/ppermute | solution.py:14
  78.5 17.1 %fusion.6 = bf16[4,2048,512]{1,2,0:T(8,128)(2,1)} fusion(bf16[4,512,2048]{2,1,0:T(8,128)(2,1)} %bitcast.51, bf16[3,512,2048]{2,1,0:T(8,128)(2,1)} %collective-permute-done, f32[512]{0:T(512)S(1)} %get-tuple-element.10, f32[512]{0:T(512)S(1)} %get-tuple-element.11, f32[512]{0:T(512)S(1)} %get-tuple-element.12, f32[512]{0:T(512)S(1)} %get-tuple-element.9, ...), kind=kOutput, calls=%fused_computation.18 | convolution fusion | flops 4388290560 | bytes 23601152 | tf_op jit(solution)/shard_map/kn,sni->ski/dot_general | solution.py:54
  95.6 0.0 copy-start.2
  95.6 8.3 %copy.7 = bf16[4,2,16,16,2048]{4,3,1,0,2:T(8,128)(2,1)} copy(bf16[4,2,16,16,2048]{4,3,2,1,0:T(8,128)(2,1)} %bitcast.50) | data formatting | bytes 16777216 | tf_op jit(solution)/shard_map/reshape | solution.py:55
  103.9 7.2 %all-to-all-start = ((bf16[4,2,16,16,2048]{4,3,1,0,2:T(8,128)(2,1)}), bf16[4,2,16,16,2048]{4,3,1,0,2:T(8,128)(2,1)}, u32[]{:S(2)}, u32[]{:S(2)}) async-start(bf16[4,2,16,16,2048]{4,3,1,0,2:T(8,128)(2,1)} %copy.7), calls=%async_computation | async-start | bytes 16777216 | tf_op jit(solution)/shard_map/all_to_all | solution.py:56
  111.1 0.0 copy-done.2
  111.1 0.1 copy.8
  111.2 0.1 reshape.85
  111.3 0.0 copy-done
  111.3 0.6 gather_fusion
  112.0 181.5 %all-to-all-done = bf16[4,2,16,16,2048]{4,3,1,0,2:T(8,128)(2,1)} async-done(((bf16[4,2,16,16,2048]{4,3,1,0,2:T(8,128)(2,1)}), bf16[4,2,16,16,2048]{4,3,1,0,2:T(8,128)(2,1)}, u32[]{:S(2)}, u32[]{:S(2)}) %all-to-all-start) | async-done | bytes 8388640 | tf_op jit(solution)/shard_map/all_to_all | solution.py:56
  293.5 26.8 %copy.9 = bf16[64,2,16,2048]{0,2,3,1:T(8,128)(2,1)} copy(bf16[64,2,16,2048]{3,2,1,0:T(8,128)(2,1)} %bitcast.7) | data formatting | bytes 16777216 | tf_op jit(solution)/shard_map/squeeze | solution.py:56
  320.3 25.9 %gather_fusion.2 = bf16[2048,64,2,16]{1,3,2,0:T(8,128)(2,1)} fusion(bf16[64,2,16,2048]{0,2,3,1:T(8,128)(2,1)} %copy.9, s32[2048]{0:T(1024)S(1)} %fusion.26), kind=kCustom, calls=%fused_computation.2 | custom fusion | bytes 16785408 | tf_op jit(solution)/shard_map/gather | solution.py:59
  346.2 25.9 %gather_fusion.1 = bf16[2048,64,2,16]{1,3,2,0:T(8,128)(2,1)} fusion(bf16[64,2,16,2048]{0,2,3,1:T(8,128)(2,1)} %copy.9, s32[2048]{0:T(1024)S(1)} %fusion.24), kind=kCustom, calls=%fused_computation.1 | custom fusion | bytes 16785408 | tf_op jit(solution)/shard_map/gather | solution.py:58
  372.0 21.0 %copy.11 = bf16[16,128,64,2,16]{1,2,3,4,0:T(8,128)(2,1)} copy(bf16[16,128,64,2,16]{2,4,3,1,0:T(8,128)(2,1)} %bitcast.49) | data formatting | bytes 16777216 | tf_op jit(solution)/shard_map/gather | solution.py:58
  393.0 21.1 %copy.15 = bf16[64,2,16,16,128]{4,0,1,2,3:T(8,128)(2,1)} copy(bf16[64,2,16,16,128]{0,2,1,4,3:T(8,128)(2,1)} %bitcast.48) | data formatting | bytes 16777216 | tf_op jit(solution)/shard_map/gather | solution.py:59
  414.1 5.8 %fusion.35 = (bf16[64,1,16,16,128]{4,0,1,2,3:T(8,128)(2,1)}, bf16[64,1,16,16,128]{4,0,1,2,3:T(8,128)(2,1)}) fusion(bf16[64,2,16,16,128]{4,0,1,2,3:T(8,128)(2,1)} %bitcast.47), kind=kLoop, calls=%fused_computation.71 | loop fusion | flops 2097152 | bytes 16777216 | tf_op jit(solution)/shard_map/slice | solution.py:60
  419.9 14.4 %convolution_bitcast_fusion.1 = f32[16,1,16,128,128]{4,3,2,0,1:T(8,128)} fusion(bf16[64,2,16,16,128]{4,0,1,2,3:T(8,128)(2,1)} %copy.15, bf16[16,128,64,2,16]{1,2,3,4,0:T(8,128)(2,1)} %copy.11), kind=kOutput, calls=%fused_computation.10 | convolution fusion | flops 1073741824 | bytes 33554432 | tf_op jit(solution)/shard_map/sckbi,sckbj->bkij/dot_general | solution.py:61
  434.3 14.9 %convolution_bitcast_fusion = f32[16,1,16,128,128]{4,3,2,0,1:T(8,128)} fusion(bf16[64,2,16,16,128]{4,0,1,2,3:T(8,128)(2,1)} %copy.15, bf16[64,1,16,16,128]{4,0,1,2,3:T(8,128)(2,1)} %get-tuple-element.6, bf16[64,1,16,16,128]{4,0,1,2,3:T(8,128)(2,1)} %get-tuple-element.5), kind=kOutput, calls=%fused_computation.9 | convolution fusion | flops 1077936128 | bytes 33554432 | tf_op jit(solution)/shard_map/sckbi,sckbj->bkij/dot_general | solution.py:62
  449.2 12.2 %maximum_multiply_fusion = f32[16,2,16,128,128]{4,3,2,0,1:T(8,128)S(1)} fusion(f32[16,1,16,128,128]{4,3,2,0,1:T(8,128)} %convolution_bitcast_fusion, f32[16,1,16,128,128]{4,3,2,0,1:T(8,128)} %convolution_bitcast_fusion.1), kind=kLoop, calls=%fused_computation.3 | loop fusion | flops 16777216 | bytes 67108864 | tf_op jit(solution)/shard_map/div | solution.py:63
  461.4 0.0 copy-start.1
  461.4 11.3 %copy.17 = f32[16,2,16,128,128]{4,3,2,1,0:T(8,128)} copy(f32[16,2,16,128,128]{4,3,2,0,1:T(8,128)S(1)} %maximum_multiply_fusion) | data formatting | bytes 67108864 | tf_op jit(solution)/shard_map/div | solution.py:63
  472.7 0.0 copy-done.1
  (6 shorter events, 0.0 us)
Async XLA Ops:
  0.0 111.3 %copy-start = (s32[2048]{0:T(1024)S(1)}, s32[2048]{0:T(1024)}, u32[]{:S(2)}) copy-start(s32[2048]{0:T(1024)} %param.4) | copy-start | bytes 24580
  6.6 71.9 %collective-permute-start = (bf16[3,512,2048]{2,1,0:T(8,128)(2,1)}, bf16[3,512,2048]{2,1,0:T(8,128)(2,1)}, u32[]{:S(2)}, u32[]{:S(2)}) collective-permute-start(bf16[3,512,2048]{2,1,0:T(8,128)(2,1)} %bitcast), channel_id=1, source_target_pairs={{0,1},{1,2},{2,3},{3,4},{4,5},{5,6},{6,7},{7,8},{8,9},{9,10},{10,1... | collective-permute-start | bytes 18874376 | tf_op jit(solution)/shard_map/ppermute | solution.py:14
  95.6 15.5 %copy-start.2 = (s32[16,2]{0,1:T(2,128)S(1)}, s32[16,2]{0,1:T(2,128)}, u32[]{:S(2)}) copy-start(s32[16,2]{0,1:T(2,128)} %param.5) | copy-start | bytes 388
  103.9 189.6 %all-to-all-start = ((bf16[4,2,16,16,2048]{4,3,1,0,2:T(8,128)(2,1)}), bf16[4,2,16,16,2048]{4,3,1,0,2:T(8,128)(2,1)}, u32[]{:S(2)}, u32[]{:S(2)}) async-start(bf16[4,2,16,16,2048]{4,3,1,0,2:T(8,128)(2,1)} %copy.7), calls=%async_computation | async-start | bytes 16777216 | tf_op jit(solution)/shard_map/all_to_all | solution.py:56
  461.4 11.3 %copy-start.1 = (s32[2048]{0:T(1024)S(1)}, s32[2048]{0:T(1024)}, u32[]{:S(2)}) copy-start(s32[2048]{0:T(1024)} %param.4) | copy-start | bytes 24580
where the time goes:
time: 474 us; the launch traced here: 473 us
  waiting for transfers between devices  246 us (52%)
  local copies, waits for them, and re-layouts  148 us (31%)
  matrix products  46.3 us (10%)
  other arithmetic  20.9 us (4%)
  starting transfers between devices  10.9 us (2%)
    all_to_all x1, waiting for transfers between devices, body(): lax.all_to_all(spectra, 'tm', split_axis=2, concat_axis=0, tiled=True)  182 us
    ppermute x1, waiting for transfers between devices, from_behind(): return lax.ppermute(block, axis, route)  64.7 us
    gather x2, local copies, waits for them, and re-layouts, body(): second = data[:, :, :, columns[:, 1]]  46.9 us
    gather x2, local copies, waits for them, and re-layouts, body(): first = data[:, :, :, columns[:, 0]]  46.9 us
    squeeze x1, local copies, waits for them, and re-layouts, body(): lax.all_to_all(spectra, 'tm', split_axis=2, concat_axis=0, tiled=True)  26.8 us
    dot_general x1, matrix products, body(): jnp.einsum('kn,sni->ski', table, filtered, preferred_element_type=jnp.flo...  17.1 us
    dot_general x1, matrix products, body(): jnp.einsum('sckbi,sckbj->bkij', flipped, second, preferred_element_type=j...  14.9 us
    dot_general x1, matrix products, body(): jnp.einsum('sckbi,sckbj->bkij', first, second, preferred_element_type=jnp...  14.4 us
  transfers between devices with their start and end apart: 2, of which 2 were waited for; matrix products, arithmetic and copies ran while one was open for 1% of the time, Pallas kernels for 0%

commit v1 on v0

--- a/solution.py
+++ b/solution.py
@@ -53,7 +53,15 @@
     table = dft_table(CHANNELS)
     spectra = jnp.einsum("kn,sni->ski", table, filtered, preferred_element_type=jnp.float32)
     spectra = spectra.astype(jnp.bfloat16).reshape(spec_dev, 2, groups, band_dev, width)
-    data = lax.all_to_all(spectra, "tm", split_axis=2, concat_axis=0, tiled=True)[:, :, 0]
+    data = jnp.concatenate(
+        lax.all_to_all(
+            jnp.stack(jnp.split(spectra, lax.axis_size("tm"), axis=2), axis=0),
+            axis_name="tm",
+            split_axis=0,
+            concat_axis=0,
+        ),
+        axis=0,
+    )[:, :, 0]
     total = data.shape[0]
     first = data[:, :, :, columns[:, 0]]
     second = data[:, :, :, columns[:, 1]]

time: 474 us -> 477 us (level)
  local copies, waits for them, and re-layouts: 148 us -> 153 us
    another operation x0 -> x2, local copies, waits for them, and re-layouts: none -> 27.6 us  [the longest x1 26.8 us: body(): jnp.concatenate(lax.all_to_all(jnp.stack(jnp.split(spectra, lax.axis_size...]
    squeeze x1 -> x0, local copies, waits for them, and re-layouts: 26.8 us -> none  [body(): lax.all_to_all(spectra, 'tm', split_axis=2, concat_axis=0, tiled=True)]
    unnamed x6 -> x21, local copies, waits for them, and re-layouts: 0.01 us -> 12.5 us
    reshape x1 -> x0, local copies, waits for them, and re-layouts: 8.28 us -> none  [body(): spectra.astype(jnp.bfloat16).reshape(spec_dev, 2, groups, band_dev, width)]
where the time goes in v1:
time: 477 us; the launch traced here: 476 us
  waiting for transfers between devices  246 us (52%)
  local copies, waits for them, and re-layouts  153 us (32%)
  matrix products  44.2 us (9%)
  other arithmetic  20.9 us (4%)
  starting transfers between devices  11.1 us (2%)
    all_to_all x1, waiting for transfers between devices, body(): lax.all_to_all(jnp.stack(jnp.split(spectra, lax.axis_size('tm'), axis=2),...  182 us
    ppermute x1, waiting for transfers between devices, from_behind(): return lax.ppermute(block, axis, route)  64.6 us
    gather x2, local copies, waits for them, and re-layouts, body(): second = data[:, :, :, columns[:, 1]]  46.9 us
    gather x2, local copies, waits for them, and re-layouts, body(): first = data[:, :, :, columns[:, 0]]  46.9 us
    another operation x1, local copies, waits for them, and re-layouts, body(): jnp.concatenate(lax.all_to_all(jnp.stack(jnp.split(spectra, lax.axis_size...  26.8 us
    dot_general x1, matrix products, body(): jnp.einsum('kn,sni->ski', table, filtered, preferred_element_type=jnp.flo...  14.9 us
    dot_general x1, matrix products, body(): jnp.einsum('sckbi,sckbj->bkij', flipped, second, preferred_element_type=j...  14.9 us
    dot_general x1, matrix products, body(): jnp.einsum('sckbi,sckbj->bkij', first, second, preferred_element_type=jnp...  14.4 us
  transfers between devices with their start and end apart: 2, of which 2 were waited for; matrix products, arithmetic and copies ran while one was open for 1% of the time, Pallas kernels for 0%

profile of v1, /device:TPU:13, one launch (start us, length us, event | category | flops | bytes accessed | tf_op | source)
XLA Modules:
  0.0 475.7 jit_solution(16743682987663693089)
XLA Ops:
  0.0 0.0 copy-start
  0.0 6.6 %slice.44 = bf16[1536,2048]{1,0:T(8,128)(2,1)} slice(bf16[2048,2048]{1,0:T(8,128)(2,1)} %param.3), slice={[512:2048], [0:2048]} | slice | bytes 12582912 | tf_op jit(solution)/shard_map/slice | solution.py:44
  6.6 3.7 collective-permute-start
  10.3 0.7 multiply_reduce_fusion
  11.7 0.1 broadcast_divide_fusion
  11.7 2.2 negate_convert_fusion
  13.9 64.6 %collective-permute-done = bf16[3,512,2048]{2,1,0:T(8,128)(2,1)} collective-permute-done((bf16[3,512,2048]{2,1,0:T(8,128)(2,1)}, bf16[3,512,2048]{2,1,0:T(8,128)(2,1)}, u32[]{:S(2)}, u32[]{:S(2)}) %collective-permute-start) | collective-permute-done | bytes 6291488 | tf_op jit(solution)/shard_map/ppermute | solution.py:14
  78.5 14.9 %fusion.6 = bf16[4,2048,512]{1,2,0:T(8,128)(2,1)S(1)} fusion(bf16[4,512,2048]{2,1,0:T(8,128)(2,1)} %bitcast.158, bf16[3,512,2048]{2,1,0:T(8,128)(2,1)} %collective-permute-done, f32[512]{0:T(512)S(1)} %get-tuple-element.10, f32[512]{0:T(512)S(1)} %get-tuple-element.11, f32[512]{0:T(512)S(1)} %get-tuple-element.12, f32[512]{0:T(512)S(1)} %get-tuple-element.9, ...), kind=kOutput, calls=%fused_computation.18 | convolution fusion | flops 4388290560 | bytes 23601152 | tf_op jit(solution)/shard_map/kn,sni->ski/dot_general | solution.py:54
  93.5 0.8 fusion.25
  94.3 0.8 fusion.24
  95.2 0.8 fusion.23
  96.0 0.8 fusion.22
  96.8 0.8 fusion.21
  97.6 0.8 fusion.20
  98.5 0.8 fusion.19
  99.3 0.8 fusion.18
  100.1 0.8 fusion.17
  101.0 0.8 fusion.16
  101.8 0.8 fusion.15
  102.6 0.8 fusion.14
  103.5 0.8 fusion.13
  104.3 0.8 fusion.12
  105.1 0.8 fusion.11
  106.0 0.8 fusion.10
  106.8 0.0 copy-start.2
  106.8 7.4 %all-to-all-start = ((bf16[16,4,2,1,16,2048]{5,4,2,1,3,0:T(8,128)(2,1)}), bf16[16,4,2,1,16,2048]{5,4,2,1,3,0:T(8,128)(2,1)}, u32[]{:S(2)}, u32[]{:S(2)}) async-start(bf16[16,4,2,1,16,2048]{5,4,2,1,3,0:T(8,128)(2,1)} %fusion.10), calls=%async_computation | async-start | bytes 16777216 | tf_op jit(solution)/shard_map/all_to_all | solution.py:57
  114.2 0.0 copy-done.2
  114.2 0.1 copy.88
  114.3 0.1 reshape.84
  114.4 0.0 copy-done
  114.4 0.6 gather_fusion
  115.0 181.5 %all-to-all-done = bf16[16,4,2,1,16,2048]{5,4,2,1,3,0:T(8,128)(2,1)} async-done(((bf16[16,4,2,1,16,2048]{5,4,2,1,3,0:T(8,128)(2,1)}), bf16[16,4,2,1,16,2048]{5,4,2,1,3,0:T(8,128)(2,1)}, u32[]{:S(2)}, u32[]{:S(2)}) %all-to-all-start) | async-done | bytes 8388640 | tf_op jit(solution)/shard_map/all_to_all | solution.py:57
  296.5 26.8 %copy.89 = bf16[64,2,16,2048]{0,2,3,1:T(8,128)(2,1)} copy(bf16[64,2,16,2048]{3,2,1,0:T(8,128)(2,1)} %bitcast.22) | data formatting | bytes 16777216 | tf_op jit(solution)/shard_map/squeeze;reshape | solution.py:56
  323.3 25.9 %gather_fusion.2 = bf16[2048,64,2,16]{1,3,2,0:T(8,128)(2,1)} fusion(bf16[64,2,16,2048]{0,2,3,1:T(8,128)(2,1)} %copy.89, s32[2048]{0:T(1024)S(1)} %get-tuple-element.16), kind=kCustom, calls=%fused_computation.2 | custom fusion | bytes 16785408 | tf_op jit(solution)/shard_map/gather | solution.py:67
  349.2 25.9 %gather_fusion.1 = bf16[2048,64,2,16]{1,3,2,0:T(8,128)(2,1)} fusion(bf16[64,2,16,2048]{0,2,3,1:T(8,128)(2,1)} %copy.89, s32[2048]{0:T(1024)S(1)} %get-tuple-element.15), kind=kCustom, calls=%fused_computation.1 | custom fusion | bytes 16785408 | tf_op jit(solution)/shard_map/gather | solution.py:66
  375.0 21.0 %copy.91 = bf16[16,128,64,2,16]{1,2,3,4,0:T(8,128)(2,1)} copy(bf16[16,128,64,2,16]{2,4,3,1,0:T(8,128)(2,1)} %bitcast.141) | data formatting | bytes 16777216 | tf_op jit(solution)/shard_map/gather | solution.py:66
  396.0 21.1 %copy.95 = bf16[64,2,16,16,128]{4,0,1,2,3:T(8,128)(2,1)} copy(bf16[64,2,16,16,128]{0,2,1,4,3:T(8,128)(2,1)} %bitcast.140) | data formatting | bytes 16777216 | tf_op jit(solution)/shard_map/gather | solution.py:67
  417.1 5.8 %fusion.51 = (bf16[64,1,16,16,128]{4,0,1,2,3:T(8,128)(2,1)}, bf16[64,1,16,16,128]{4,0,1,2,3:T(8,128)(2,1)}) fusion(bf16[64,2,16,16,128]{4,0,1,2,3:T(8,128)(2,1)} %bitcast.139), kind=kLoop, calls=%fused_computation.103 | loop fusion | flops 2097152 | bytes 16777216 | tf_op jit(solution)/shard_map/slice | solution.py:68
  422.9 14.4 %convolution_bitcast_fusion.1 = f32[16,1,16,128,128]{4,3,2,0,1:T(8,128)} fusion(bf16[64,2,16,16,128]{4,0,1,2,3:T(8,128)(2,1)} %copy.95, bf16[16,128,64,2,16]{1,2,3,4,0:T(8,128)(2,1)} %copy.91), kind=kOutput, calls=%fused_computation.10 | convolution fusion | flops 1073741824 | bytes 33554432 | tf_op jit(solution)/shard_map/sckbi,sckbj->bkij/dot_general | solution.py:69
  437.3 14.9 %convolution_bitcast_fusion = f32[16,1,16,128,128]{4,3,2,0,1:T(8,128)} fusion(bf16[64,2,16,16,128]{4,0,1,2,3:T(8,128)(2,1)} %copy.95, bf16[64,1,16,16,128]{4,0,1,2,3:T(8,128)(2,1)} %get-tuple-element.6, bf16[64,1,16,16,128]{4,0,1,2,3:T(8,128)(2,1)} %get-tuple-element.5), kind=kOutput, calls=%fused_computation.9 | convolution fusion | flops 1077936128 | bytes 33554432 | tf_op jit(solution)/shard_map/sckbi,sckbj->bkij/dot_general | solution.py:70
  452.2 12.2 %maximum_multiply_fusion = f32[16,2,16,128,128]{4,3,2,0,1:T(8,128)S(1)} fusion(f32[16,1,16,128,128]{4,3,2,0,1:T(8,128)} %convolution_bitcast_fusion, f32[16,1,16,128,128]{4,3,2,0,1:T(8,128)} %convolution_bitcast_fusion.1), kind=kLoop, calls=%fused_computation.3 | loop fusion | flops 16777216 | bytes 67108864 | tf_op jit(solution)/shard_map/div | solution.py:71
  464.4 0.0 copy-start.1
  464.4 11.3 %copy.97 = f32[16,2,16,128,128]{4,3,2,1,0:T(8,128)} copy(f32[16,2,16,128,128]{4,3,2,0,1:T(8,128)S(1)} %maximum_multiply_fusion) | data formatting | bytes 67108864 | tf_op jit(solution)/shard_map/div | solution.py:71
  475.7 0.0 copy-done.1
  (5 shorter events, 0.0 us)
Async XLA Ops:
  0.0 114.4 %copy-start = (s32[2048]{0:T(1024)S(1)}, s32[2048]{0:T(1024)}, u32[]{:S(2)}) copy-start(s32[2048]{0:T(1024)} %param.4) | copy-start | bytes 24580
  6.6 71.9 %collective-permute-start = (bf16[3,512,2048]{2,1,0:T(8,128)(2,1)}, bf16[3,512,2048]{2,1,0:T(8,128)(2,1)}, u32[]{:S(2)}, u32[]{:S(2)}) collective-permute-start(bf16[3,512,2048]{2,1,0:T(8,128)(2,1)} %bitcast), channel_id=1, source_target_pairs={{0,1},{1,2},{2,3},{3,4},{4,5},{5,6},{6,7},{7,8},{8,9},{9,10},{10,1... | collective-permute-start | bytes 18874376 | tf_op jit(solution)/shard_map/ppermute | solution.py:14
  106.8 7.4 %copy-start.2 = (s32[16,2]{0,1:T(2,128)S(1)}, s32[16,2]{0,1:T(2,128)}, u32[]{:S(2)}) copy-start(s32[16,2]{0,1:T(2,128)} %param.5) | copy-start | bytes 388
  106.8 189.7 %all-to-all-start = ((bf16[16,4,2,1,16,2048]{5,4,2,1,3,0:T(8,128)(2,1)}), bf16[16,4,2,1,16,2048]{5,4,2,1,3,0:T(8,128)(2,1)}, u32[]{:S(2)}, u32[]{:S(2)}) async-start(bf16[16,4,2,1,16,2048]{5,4,2,1,3,0:T(8,128)(2,1)} %fusion.10), calls=%async_computation | async-start | bytes 16777216 | tf_op jit(solution)/shard_map/all_to_all | solution.py:57
  464.4 11.3 %copy-start.1 = (s32[2048]{0:T(1024)S(1)}, s32[2048]{0:T(1024)}, u32[]{:S(2)}) copy-start(s32[2048]{0:T(1024)} %param.4) | copy-start | bytes 24580
